TPU v7x, 256 devices: a whole 4x4x8 slice. The times are simulated.
256 devices in a mesh: rows: 8 (over y, x_lo), cols: 32 (over z, x_hi, core).
Axes of the slice: x: 4 (x_hi: 2, x_lo: 2; x = x_hi * 2 + x_lo), y: 4, z: 8, core: 2. Of those that a mesh axis runs over, the one named last changes fastest.
Arguments:
- counts: bfloat16 [4096, 262144], P('rows', 'cols'), may hold values from 0 to 12, as said below
- start_a: float32 [4096, 128], P(('rows', 'cols')), may hold values from -0.4 to 0.4
- start_b: float32 [16384, 128], P(('cols', 'rows')), may hold values from -0.4 to 0.4
- start_c: float32 [16, 128], replicated, may hold values from -0.4 to 0.4
Outputs:
- factor_a: float32 [4096, 128], P(('rows', 'cols'))
- factor_b: float32 [16384, 128], P(('cols', 'rows'))
- factor_c: float32 [16, 128], replicated
Inputs may be any that keep to these rules, and one draw needn't show every extreme that they name: counts holds whole numbers.
All inputs are finite; a program needn't handle non-finite values.
Results may differ from a plain program's by a relative error of at most 0.009.
Values may be sent and summed in bfloat16 or wider, within the bound.
No kernel may reach another device: no remote copies, remote signals or barrier semaphores. Data moves between devices by JAX's collectives and lax.ppermute only.
A program may use at most 128 MiB of HBM per device.

v0:
```python
import math
import jax
import jax.numpy as jnp
from jax import lax
from jax.sharding import PartitionSpec as P

ITERS = 2


def local(counts, start_a, start_b, start_c):
    rows_here, flat_width = counts.shape
    depth = start_c.shape[0]
    cols_here = flat_width // depth
    total_i = rows_here * lax.axis_size("rows")
    total_j = cols_here * lax.axis_size("cols")
    rate_a = 0.3 / math.sqrt(total_j * depth)
    rate_b = 0.3 / math.sqrt(total_i * depth)
    rate_c = 0.3 / math.sqrt(total_i * total_j)
    local_a, local_b, shared_c = (start_a, start_b, start_c)
    for iteration in range(ITERS):
        low_a = lax.all_gather(local_a.astype(jnp.bfloat16), "cols", axis=0, tiled=True)
        low_b = lax.all_gather(local_b.astype(jnp.bfloat16), "rows", axis=0, tiled=True)
        low_b_wide = low_b.astype(jnp.float32)
        scaled = (low_b_wide[:, None, :] * shared_c[None, :, :]).astype(jnp.bfloat16)
        scaled = scaled.reshape(cols_here * depth, shared_c.shape[1])
        log_rate = lax.dot_general(
            low_a, scaled, (((1,), (1,)), ((), ())), preferred_element_type=jnp.float32
        )
        residual = (jnp.exp(log_rate) - counts.astype(jnp.float32)).astype(jnp.bfloat16)
        grad_a = jnp.dot(residual, scaled, preferred_element_type=jnp.float32)
        mixed = lax.dot_general(
            residual, low_a, (((0,), (0,)), ((), ())), preferred_element_type=jnp.float32
        )
        mixed = mixed.reshape(cols_here, depth, shared_c.shape[1])
        grad_b = jnp.sum(mixed * shared_c[None, :, :], axis=1)
        grad_c = jnp.sum(mixed * low_b_wide[:, None, :], axis=0)
        summed_a = lax.psum_scatter(grad_a, "cols", scatter_dimension=0, tiled=True)
        summed_b = lax.psum_scatter(grad_b, "rows", scatter_dimension=0, tiled=True)
        local_a = local_a - rate_a * summed_a
        local_b = local_b - rate_b * summed_b
        summed_c = lax.psum(grad_c, ("rows", "cols"))
        shared_c = shared_c - rate_c * summed_c
    return (local_a, local_b, shared_c)


def solution(mesh):
    placed = (P("rows", "cols"), P(("rows", "cols"), None), P(("cols", "rows"), None), P())
    return jax.shard_map(
        local,
        mesh=mesh,
        in_specs=placed,
        out_specs=(P(("rows", "cols"), None), P(("cols", "rows"), None), P()),
        check_vma=False,
    )
```

profile of v0, /device:TPU:32, one launch (start us, length us, event | category | flops | bytes accessed | tf_op | source)
XLA Modules:
  0.0 455.2 jit_solution(1326504930640590621)
XLA Ops:
  7.2 0.0 copy-start.2
  7.2 0.0 copy-start.4
  7.2 0.0 copy-start.5
  7.2 0.0 reduce-scatter.5.cloned.1.call-start
  7.2 12.0 %copy.7 = bf16[512,8192]{0,1:T(8,128)(2,1)} copy(bf16[512,8192]{1,0:T(8,128)(2,1)} %param.4) | data formatting | bytes 16777216 | tf_op args[0]
  19.2 0.0 copy-done.2
  19.2 28.6 %all_gather.12 = bf16[512,128]{1,0:T(8,128)(2,1)S(1)} all-gather(bf16[64,128]{1,0:T(8,128)(2,1)S(1)} %convert_element_type.42), channel_id=1, replica_groups=mesh['rows'=8,'cols'=32] {'rows'}, dimensions={0}, use_global_device_ids=true | all-gather | bytes 147456 | tf_op jit(solution)/shard_map/all_gather | solution.py:22
  47.9 0.0 copy-done.4
  47.9 42.5 %all_gather.13 = bf16[512,128]{1,0:T(8,128)(2,1)S(1)} all-gather(bf16[16,128]{1,0:T(8,128)(2,1)S(1)} %convert_element_type.46), channel_id=1, replica_groups=mesh['rows'=8,'cols'=32] {'cols'}, dimensions={0}, use_global_device_ids=true | all-gather | bytes 135168 | tf_op jit(solution)/shard_map/all_gather | solution.py:21
  90.4 0.0 copy-done.5
  90.4 0.4 multiply_convert_fusion.1
  90.8 5.0 %fusion = bf16[512,8192]{0,1:T(8,128)(2,1)S(1)} fusion(bf16[512,8192]{0,1:T(8,128)(2,1)} %copy.7, bf16[8192,128]{1,0:T(8,128)(2,1)S(1)} %bitcast.22, bf16[512,128]{1,0:T(8,128)(2,1)S(1)} %all_gather.13), kind=kOutput, calls=%fused_computation.2 | convolution fusion | flops 1086324736 | bytes 19005440 | tf_op jit(solution)/shard_map/dot_general | solution.py:26
  95.8 0.0 copy-start
  95.8 3.2 copy-done
  99.0 3.0 fusion.4
  102.1 0.0 reduce-scatter.5.cloned.1.call-update
  102.1 0.0 reduce-scatter.7.cloned.1.call-start
  102.1 8.4 %multiply_reduce_fusion.3 = (f32[512,128]{1,0:T(8,128)}, f32[8192,128]{1,0:T(8,128)}) fusion(f32[16,128]{1,0:T(8,128)S(1)} %copy-done.5, bf16[512,8192]{0,1:T(8,128)(2,1)} %copy-done, bf16[512,128]{1,0:T(8,128)(2,1)S(1)} %all_gather.13), kind=kOutput, calls=%fused_computation.8 | convolution fusion | flops 1075773440 | bytes 12984320 | tf_op jit(solution)/shard_map/dot_general | solution.py:31
  110.5 0.0 reduce-scatter.7.cloned.1.call-update
  110.5 0.0 reduce-scatter.9.cloned.1.call-start
  110.6 2.8 multiply_reduce_fusion.2
  113.4 77.1 %psum.14 = f32[16,128]{1,0:T(8,128)S(1)} all-reduce(f32[16,128]{1,0:T(8,128)S(1)} %multiply_reduce_fusion.2), channel_id=1, replica_groups=mesh['rows'=8,'cols'=32] {'rows','cols'}, use_global_device_ids=true, to_apply=%region_4.0 | all-reduce | flops 2048 | bytes 16384 | tf_op jit(solution)/shard_map/psum | solution.py:41
  190.5 21.8 %reduce-scatter.5.cloned.1.call-done = f32[16,128]{1,0:T(8,128)} async-done(((f32[512,128]{1,0:T(8,128)}), f32[16,128]{1,0:T(8,128)}) %reduce-scatter.5.cloned.1.call-update) | async-done | bytes 8208 | tf_op jit(solution)/shard_map/reduce_scatter | solution.py:37
  212.3 0.7 fusion.3
  213.0 38.0 %all_gather.14 = bf16[512,128]{1,0:T(8,128)(2,1)S(1)} all-gather(bf16[16,128]{1,0:T(8,128)(2,1)S(1)} %fusion.3), channel_id=1, replica_groups=mesh['rows'=8,'cols'=32] {'cols'}, dimensions={0}, use_global_device_ids=true | all-gather | bytes 135168 | tf_op jit(solution)/shard_map/all_gather | solution.py:21
  251.0 2.8 reduce-scatter.7.cloned.1.call-done
  253.8 0.8 fusion.2
  254.6 28.5 %all_gather.15 = bf16[512,128]{1,0:T(8,128)(2,1)S(1)} all-gather(bf16[64,128]{1,0:T(8,128)(2,1)S(1)} %fusion.2), channel_id=1, replica_groups=mesh['rows'=8,'cols'=32] {'rows'}, dimensions={0}, use_global_device_ids=true | all-gather | bytes 147456 | tf_op jit(solution)/shard_map/all_gather | solution.py:22
  283.1 0.4 multiply_convert_fusion
  283.5 5.0 %fusion.1 = bf16[512,8192]{0,1:T(8,128)(2,1)S(1)} fusion(bf16[512,8192]{0,1:T(8,128)(2,1)} %copy.7, bf16[512,128]{1,0:T(8,128)(2,1)S(1)} %all_gather.14, bf16[8192,128]{1,0:T(8,128)(2,1)S(1)} %bitcast.24), kind=kOutput, calls=%fused_computation.3 | convolution fusion | flops 1086324736 | bytes 19005440 | tf_op jit(solution)/shard_map/dot_general | solution.py:26
  288.5 0.0 copy-start.1
  288.5 3.2 copy-done.1
  291.7 3.1 fusion.5
  294.8 0.0 reduce-scatter.9.cloned.1.call-update
  294.8 0.0 reduce-scatter.11.cloned.1.call-start
  294.9 8.4 %multiply_reduce_fusion.1 = (f32[512,128]{1,0:T(8,128)}, f32[8192,128]{1,0:T(8,128)}) fusion(f32[16,128]{1,0:T(8,128)S(1)} %multiply_subtract_fusion.4, bf16[512,8192]{0,1:T(8,128)(2,1)} %copy-done.1, bf16[512,128]{1,0:T(8,128)(2,1)S(1)} %all_gather.14), kind=kOutput, calls=%fused_computation.5 | convolution fusion | flops 1075773440 | bytes 12984320 | tf_op jit(solution)/shard_map/dot_general | solution.py:31
  303.3 0.0 copy-start.6
  303.3 0.0 copy-start.3
  303.3 0.0 reduce-scatter.11.cloned.1.call-update
  303.3 2.8 multiply_reduce_fusion
  306.1 73.2 %psum.15 = f32[16,128]{1,0:T(8,128)S(1)} all-reduce(f32[16,128]{1,0:T(8,128)S(1)} %multiply_reduce_fusion), channel_id=1, replica_groups=mesh['rows'=8,'cols'=32] {'rows','cols'}, use_global_device_ids=true, to_apply=%region_9.0 | all-reduce | flops 2048 | bytes 16384 | tf_op jit(solution)/shard_map/psum | solution.py:41
  379.4 0.6 multiply_subtract_fusion.2
  380.0 25.9 %reduce-scatter.9.cloned.1.call-done = f32[16,128]{1,0:T(8,128)} async-done(((f32[512,128]{1,0:T(8,128)}), f32[16,128]{1,0:T(8,128)}) %reduce-scatter.9.cloned.1.call-update) | async-done | bytes 8208 | tf_op jit(solution)/shard_map/reduce_scatter | solution.py:37
  405.9 0.0 copy-done.6
  405.9 1.3 multiply_subtract_fusion.3
  407.2 40.1 %reduce-scatter.11.cloned.1.call-done = f32[64,128]{1,0:T(8,128)} async-done(((f32[512,128]{1,0:T(8,128)}), f32[64,128]{1,0:T(8,128)}) %reduce-scatter.11.cloned.1.call-update) | async-done | bytes 32784 | tf_op jit(solution)/shard_map/reduce_scatter | solution.py:38
  447.3 0.0 copy-done.3
  447.3 1.4 multiply_subtract_fusion
  (5 shorter events, 0.0 us)
Async XLA Ops:
  7.2 12.0 %copy-start.2 = (f32[64,128]{1,0:T(8,128)S(1)}, f32[64,128]{1,0:T(8,128)}, u32[]{:S(2)}) copy-start(f32[64,128]{1,0:T(8,128)} %param.6) | copy-start | bytes 98308
  7.2 40.7 %copy-start.4 = (f32[16,128]{1,0:T(8,128)S(1)}, f32[16,128]{1,0:T(8,128)}, u32[]{:S(2)}) copy-start(f32[16,128]{1,0:T(8,128)} %param.5) | copy-start | bytes 24580
  7.2 83.2 %copy-start.5 = (f32[16,128]{1,0:T(8,128)S(1)}, f32[16,128]{1,0:T(8,128)}, u32[]{:S(2)}) copy-start(f32[16,128]{1,0:T(8,128)} %param.7) | copy-start | bytes 24580
  7.2 205.1 %reduce-scatter.5.cloned.1.call-start = ((), (), s32[]{:S(2)}) async-start(), calls=%async_computation.4 | async-start | bytes 270336 | tf_op jit(solution)/shard_map/reduce_scatter | solution.py:37
  95.8 3.2 copy-start
  102.1 151.7 %reduce-scatter.7.cloned.1.call-start = ((), (), s32[]{:S(2)}) async-start(), calls=%async_computation.5 | async-start | bytes 294912 | tf_op jit(solution)/shard_map/reduce_scatter | solution.py:38
  110.5 295.3 %reduce-scatter.9.cloned.1.call-start = ((), (), s32[]{:S(2)}) async-start(), calls=%async_computation.6 | async-start | bytes 270336 | tf_op jit(solution)/shard_map/reduce_scatter | solution.py:37
  288.5 3.2 copy-start.1
  294.8 152.5 %reduce-scatter.11.cloned.1.call-start = ((), (), s32[]{:S(2)}) async-start(), calls=%async_computation.7 | async-start | bytes 294912 | tf_op jit(solution)/shard_map/reduce_scatter | solution.py:38
  303.3 102.6 %copy-start.6 = (f32[16,128]{1,0:T(8,128)S(1)}, f32[16,128]{1,0:T(8,128)}, u32[]{:S(2)}) copy-start(f32[16,128]{1,0:T(8,128)} %reduce-scatter.5.cloned.1.call-done) | copy-start | bytes 24580
  303.3 144.0 %copy-start.3 = (f32[64,128]{1,0:T(8,128)S(1)}, f32[64,128]{1,0:T(8,128)}, u32[]{:S(2)}) copy-start(f32[64,128]{1,0:T(8,128)} %reduce-scatter.7.cloned.1.call-done) | copy-start | bytes 98308
Sparse Core Ops, SparseCore 0:
  102.2 110.0 reduce-scatter.4
  214.8 38.9 reduce-scatter.6
  294.9 110.8 reduce-scatter.8
  408.4 38.8 reduce-scatter.10
where the time goes:
time: 456 us; the launch traced here: 455 us
  blocking collectives  288 us (63%)
  waiting for transfers between devices  90.7 us (20%)
  matrix products  33 us (7%)
  local copies, waits for them, and re-layouts  18.4 us (4%)
  between operations  13.9 us (3%)
  other arithmetic  11.1 us (2%)
    psum x2, blocking collectives, local(): summed_c = lax.psum(grad_c, ('rows', 'cols'))  150 us
    all_gather x2, blocking collectives, local(): lax.all_gather(local_a.astype(jnp.bfloat16), 'cols', axis=0, tiled=True)  80.5 us
    all_gather x2, blocking collectives, local(): lax.all_gather(local_b.astype(jnp.bfloat16), 'rows', axis=0, tiled=True)  57.1 us
    reduce_scatter x2, waiting for transfers between devices, local(): summed_a = lax.psum_scatter(grad_a, 'cols', scatter_dimension=0, tiled=True)  47.7 us
    reduce_scatter x2, waiting for transfers between devices, local(): summed_b = lax.psum_scatter(grad_b, 'rows', scatter_dimension=0, tiled=True)  42.9 us
    unnamed x15, local copies, waits for them, and re-layouts  18.4 us
    dot_general x2, matrix products, local(): lax.dot_general(residual, low_a, (((0,), (0,)), ((), ())), preferred_elem...  16.8 us
    dot_general x2, matrix products, local(): lax.dot_general(low_a, scaled, (((1,), (1,)), ((), ())), preferred_elemen...  10.1 us
  transfers between devices with their start and end apart: 4, of which 4 were waited for; matrix products, arithmetic and copies ran while one was open for 5% of the time, Pallas kernels for 0%

commit v1 on v0

--- a/solution.py
+++ b/solution.py
@@ -18,7 +18,11 @@
     rate_c = 0.3 / math.sqrt(total_i * total_j)
     local_a, local_b, shared_c = (start_a, start_b, start_c)
     for iteration in range(ITERS):
-        low_a = lax.all_gather(local_a.astype(jnp.bfloat16), "cols", axis=0, tiled=True)
+        view = local_a.astype(jnp.bfloat16)
+        out_arr = lax.axis_size("cols")
+        tmp = jnp.stack([view] * out_arr)
+        small = lax.all_to_all(tmp, "cols", 0, 0)
+        low_a = jnp.concatenate(small, axis=0)
         low_b = lax.all_gather(local_b.astype(jnp.bfloat16), "rows", axis=0, tiled=True)
         low_b_wide = low_b.astype(jnp.float32)
         scaled = (low_b_wide[:, None, :] * shared_c[None, :, :]).astype(jnp.bfloat16)

time: 456 us -> 433 us (0.950)
  blocking collectives: 288 us -> 206 us
  waiting for transfers between devices: 90.7 us -> 120 us
  starting transfers between devices: 0.16 us -> 18.7 us
  matrix products: 33 us -> 43.2 us
    all_gather x2 -> x0, blocking collectives: 80.5 us -> none  [local(): lax.all_gather(local_a.astype(jnp.bfloat16), 'cols', axis=0, tiled=True)]
    reduce_scatter x2, waiting for transfers between devices: 42.9 us -> 72.9 us  [local(): summed_b = lax.psum_scatter(grad_b, 'rows', scatter_dimension=0, tiled=True)]
    all_to_all x0 -> x2, starting transfers between devices: none -> 18.4 us  [local(): small = lax.all_to_all(tmp, 'cols', 0, 0)]
    dot_general x2, matrix products: 16.8 us -> 27.1 us  [local(): lax.dot_general(residual, low_a, (((0,), (0,)), ((), ())), preferred_elem...]
    reduce_sum x2 -> x0, other arithmetic: 5.57 us -> none  [local(): grad_c = jnp.sum(mixed * low_b_wide[:, None, :], axis=0)]
  transfers between devices with their start and end apart: 4 -> 6, of which waited for: 4 -> 4; matrix products, arithmetic and copies ran while one was open for 5% -> 11% of each run, Pallas kernels for 0% -> 0%
where the time goes in v1:
time: 433 us; the launch traced here: 432 us
  blocking collectives  206 us (48%)
  waiting for transfers between devices  120 us (28%)
  matrix products  43.2 us (10%)
  local copies, waits for them, and re-layouts  22.5 us (5%)
  starting transfers between devices  18.7 us (4%)
  between operations  13.9 us (3%)
  other arithmetic  7.91 us (2%)
    psum x2, blocking collectives, local(): summed_c = lax.psum(grad_c, ('rows', 'cols'))  148 us
    reduce_scatter x2, waiting for transfers between devices, local(): summed_b = lax.psum_scatter(grad_b, 'rows', scatter_dimension=0, tiled=True)  72.9 us
    all_gather x2, blocking collectives, local(): lax.all_gather(local_b.astype(jnp.bfloat16), 'rows', axis=0, tiled=True)  57.3 us
    reduce_scatter x2, waiting for transfers between devices, local(): summed_a = lax.psum_scatter(grad_a, 'cols', scatter_dimension=0, tiled=True)  47.5 us
    dot_general x2, matrix products, local(): lax.dot_general(residual, low_a, (((0,), (0,)), ((), ())), preferred_elem...  27.1 us
    unnamed x15, local copies, waits for them, and re-layouts  18.4 us
    all_to_all x2, starting transfers between devices, local(): small = lax.all_to_all(tmp, 'cols', 0, 0)  18.4 us
    dot_general x2, matrix products, local(): lax.dot_general(low_a, scaled, (((1,), (1,)), ((), ())), preferred_elemen...  9.99 us
  transfers between devices with their start and end apart: 6, of which 4 were waited for; matrix products, arithmetic and copies ran while one was open for 11% of the time, Pallas kernels for 0%

profile of v1, /device:TPU:32, one launch (start us, length us, event | category | flops | bytes accessed | tf_op | source)
XLA Modules:
  0.0 432.4 jit_solution(14409933941166641745)
XLA Ops:
  7.2 0.7 convert_element_type.60
  7.9 0.7 stack.4
  8.5 11.2 %all-to-all-start = ((bf16[32,16,128]{2,1,0:T(8,128)(2,1)}), bf16[32,16,128]{2,1,0:T(8,128)(2,1)S(1)}, u32[]{:S(2)}, u32[]{:S(2)}) async-start(bf16[32,16,128]{2,1,0:T(8,128)(2,1)} %stack.4), calls=%async_computation | async-start | bytes 262144 | tf_op jit(solution)/shard_map/all_to_all | solution.py:24
  19.7 0.0 reduce-scatter.5.cloned.1.call-start
  19.8 0.8 convert_element_type.56
  20.6 28.6 %all_gather.6 = bf16[512,128]{1,0:T(8,128)(2,1)S(1)} all-gather(bf16[64,128]{1,0:T(8,128)(2,1)S(1)} %convert_element_type.56), channel_id=1, replica_groups=mesh['rows'=8,'cols'=32] {'rows'}, dimensions={0}, use_global_device_ids=true | all-gather | bytes 147456 | tf_op jit(solution)/shard_map/all_gather | solution.py:26
  49.2 1.2 multiply_convert_fusion.1
  50.4 1.4 copy.11
  51.7 12.0 %copy.12 = bf16[512,8192]{0,1:T(8,128)(2,1)} copy(bf16[512,8192]{1,0:T(8,128)(2,1)} %param.4) | data formatting | bytes 16777216 | tf_op args[0]
  63.7 0.0 all-to-all-done
  63.7 5.0 %fusion = bf16[512,8192]{0,1:T(8,128)(2,1)S(1)} fusion(bf16[512,8192]{0,1:T(8,128)(2,1)} %copy.12, bf16[8192,128]{1,0:T(8,128)(2,1)S(1)} %bitcast.27, bf16[512,128]{1,0:T(8,128)(2,1)S(1)} %bitcast.34), kind=kOutput, calls=%fused_computation.2 | convolution fusion | flops 1086324736 | bytes 19005440 | tf_op jit(solution)/shard_map/dot_general | solution.py:30
  68.7 0.0 copy-start
  68.7 3.2 copy-done
  71.9 0.0 copy-start.5
  71.9 3.1 fusion.8
  75.0 0.0 reduce-scatter.5.cloned.1.call-update
  75.0 0.2 reduce-scatter.7.cloned.1.call-start
  75.2 0.0 copy-done.5
  75.2 0.0 copy-start.4
  75.3 0.0 copy-start.2
  75.3 13.5 %multiply_reduce_fusion.3 = (f32[512,128]{1,0:T(8,128)}, f32[16,128]{1,0:T(8,128)S(1)}) fusion(f32[16,128]{1,0:T(8,128)S(1)} %copy-done.5, f32[512,128]{1,0:T(8,128)S(1)} %convert_element_type.57, bf16[512,128,1]{1,0,2:T(8,128)(2,1)S(1)} %bitcast.35, bf16[512,16,512]{2,1,0:T(8,128)(2,1)} %bitcast.26), kind=kOutput, calls=%fused_computation.12 | convolution fusion | flops 1077868544 | bytes 9060352 | tf_op jit(solution)/shard_map/dot_general | solution.py:35
  88.8 0.0 reduce-scatter.7.cloned.1.call-update
  88.8 75.3 %psum.14 = f32[16,128]{1,0:T(8,128)S(1)} all-reduce(f32[16,128]{1,0:T(8,128)S(1)} %get-tuple-element.6), channel_id=1, replica_groups=mesh['rows'=8,'cols'=32] {'rows','cols'}, use_global_device_ids=true, to_apply=%region_4.0 | all-reduce | flops 2048 | bytes 16384 | tf_op jit(solution)/shard_map/psum | solution.py:45
  164.2 24.0 %reduce-scatter.5.cloned.1.call-done = f32[16,128]{1,0:T(8,128)} async-done(((f32[512,128]{1,0:T(8,128)}), f32[16,128]{1,0:T(8,128)}) %reduce-scatter.5.cloned.1.call-update) | async-done | bytes 8208 | tf_op jit(solution)/shard_map/reduce_scatter | solution.py:41
  188.1 0.0 copy-done.4
  188.1 0.7 fusion.7
  188.8 0.7 stack.5
  189.5 7.2 %all-to-all-start.1 = ((bf16[32,16,128]{2,1,0:T(8,128)(2,1)}), bf16[32,16,128]{2,1,0:T(8,128)(2,1)S(1)}, u32[]{:S(2)}, u32[]{:S(2)}) async-start(bf16[32,16,128]{2,1,0:T(8,128)(2,1)} %stack.5), calls=%async_computation.2 | async-start | bytes 262144 | tf_op jit(solution)/shard_map/all_to_all | solution.py:24
  196.7 0.0 reduce-scatter.9.cloned.1.call-start
  196.8 32.8 %reduce-scatter.7.cloned.1.call-done = f32[64,128]{1,0:T(8,128)} async-done(((f32[512,128]{1,0:T(8,128)}), f32[64,128]{1,0:T(8,128)}) %reduce-scatter.7.cloned.1.call-update) | async-done | bytes 32784 | tf_op jit(solution)/shard_map/reduce_scatter | solution.py:42
  229.5 0.0 copy-done.2
  229.5 0.8 fusion.6
  230.3 28.7 %all_gather.7 = bf16[512,128]{1,0:T(8,128)(2,1)S(1)} all-gather(bf16[64,128]{1,0:T(8,128)(2,1)S(1)} %fusion.6), channel_id=1, replica_groups=mesh['rows'=8,'cols'=32] {'rows'}, dimensions={0}, use_global_device_ids=true | all-gather | bytes 147456 | tf_op jit(solution)/shard_map/all_gather | solution.py:26
  259.0 0.5 multiply_convert_fusion
  259.5 1.4 copy.14
  260.8 0.0 all-to-all-done.1
  260.8 5.0 %fusion.1 = bf16[512,8192]{0,1:T(8,128)(2,1)S(1)} fusion(bf16[512,8192]{0,1:T(8,128)(2,1)} %copy.12, bf16[512,128]{1,0:T(8,128)(2,1)S(1)} %bitcast.32, bf16[8192,128]{1,0:T(8,128)(2,1)S(1)} %bitcast.30), kind=kOutput, calls=%fused_computation.3 | convolution fusion | flops 1086324736 | bytes 19005440 | tf_op jit(solution)/shard_map/dot_general | solution.py:30
  265.8 0.0 copy-start.1
  265.8 3.2 copy-done.1
  269.1 3.1 fusion.9
  272.1 0.0 reduce-scatter.9.cloned.1.call-update
  272.1 0.0 reduce-scatter.11.cloned.1.call-start
  272.2 0.0 copy-start.6
  272.2 0.0 copy-start.3
  272.2 13.6 %multiply_reduce_fusion = (f32[16,128]{1,0:T(8,128)S(1)}, f32[512,128]{1,0:T(8,128)}) fusion(f32[512,128]{1,0:T(8,128)S(1)} %convert_element_type.65, f32[16,128]{1,0:T(8,128)S(1)} %multiply_subtract_fusion.4, bf16[512,128,1]{1,0,2:T(8,128)(2,1)S(1)} %bitcast.33, bf16[512,16,512]{2,1,0:T(8,128)(2,1)} %bitcast.29), kind=kOutput, calls=%fused_computation.8 | convolution fusion | flops 1077868544 | bytes 9060352 | tf_op jit(solution)/shard_map/dot_general | solution.py:35
  285.8 0.0 reduce-scatter.11.cloned.1.call-update
  285.8 73.1 %psum.15 = f32[16,128]{1,0:T(8,128)S(1)} all-reduce(f32[16,128]{1,0:T(8,128)S(1)} %get-tuple-element.3), channel_id=1, replica_groups=mesh['rows'=8,'cols'=32] {'rows','cols'}, use_global_device_ids=true, to_apply=%region_9.0 | all-reduce | flops 2048 | bytes 16384 | tf_op jit(solution)/shard_map/psum | solution.py:45
  358.9 0.6 multiply_subtract_fusion.2
  359.5 23.6 %reduce-scatter.9.cloned.1.call-done = f32[16,128]{1,0:T(8,128)} async-done(((f32[512,128]{1,0:T(8,128)}), f32[16,128]{1,0:T(8,128)}) %reduce-scatter.9.cloned.1.call-update) | async-done | bytes 8208 | tf_op jit(solution)/shard_map/reduce_scatter | solution.py:41
  383.1 0.0 copy-done.6
  383.1 1.3 multiply_subtract_fusion.3
  384.4 40.1 %reduce-scatter.11.cloned.1.call-done = f32[64,128]{1,0:T(8,128)} async-done(((f32[512,128]{1,0:T(8,128)}), f32[64,128]{1,0:T(8,128)}) %reduce-scatter.11.cloned.1.call-update) | async-done | bytes 32784 | tf_op jit(solution)/shard_map/reduce_scatter | solution.py:42
  424.5 0.0 copy-done.3
  424.5 1.4 multiply_subtract_fusion
  (3 shorter events, 0.0 us)
Async XLA Ops:
  8.5 55.2 %all-to-all-start = ((bf16[32,16,128]{2,1,0:T(8,128)(2,1)}), bf16[32,16,128]{2,1,0:T(8,128)(2,1)S(1)}, u32[]{:S(2)}, u32[]{:S(2)}) async-start(bf16[32,16,128]{2,1,0:T(8,128)(2,1)} %stack.4), calls=%async_computation | async-start | bytes 262144 | tf_op jit(solution)/shard_map/all_to_all | solution.py:24
  19.7 168.4 %reduce-scatter.5.cloned.1.call-start = ((), (), s32[]{:S(2)}) async-start(), calls=%async_computation.6 | async-start | bytes 270336 | tf_op jit(solution)/shard_map/reduce_scatter | solution.py:41
  68.7 3.2 copy-start
  71.9 3.3 copy-start.5
  75.0 154.5 %reduce-scatter.7.cloned.1.call-start = ((), (), s32[]{:S(2)}) async-start(), calls=%async_computation.7 | async-start | bytes 294912 | tf_op jit(solution)/shard_map/reduce_scatter | solution.py:42
  75.2 112.9 %copy-start.4 = (f32[16,128]{1,0:T(8,128)S(1)}, f32[16,128]{1,0:T(8,128)}, u32[]{:S(2)}) copy-start(f32[16,128]{1,0:T(8,128)} %param.5) | copy-start | bytes 24580
  75.3 154.3 %copy-start.2 = (f32[64,128]{1,0:T(8,128)S(1)}, f32[64,128]{1,0:T(8,128)}, u32[]{:S(2)}) copy-start(f32[64,128]{1,0:T(8,128)} %param.6) | copy-start | bytes 98308
  189.5 71.3 %all-to-all-start.1 = ((bf16[32,16,128]{2,1,0:T(8,128)(2,1)}), bf16[32,16,128]{2,1,0:T(8,128)(2,1)S(1)}, u32[]{:S(2)}, u32[]{:S(2)}) async-start(bf16[32,16,128]{2,1,0:T(8,128)(2,1)} %stack.5), calls=%async_computation.2 | async-start | bytes 262144 | tf_op jit(solution)/shard_map/all_to_all | solution.py:24
  196.7 186.4 %reduce-scatter.9.cloned.1.call-start = ((), (), s32[]{:S(2)}) async-start(), calls=%async_computation.8 | async-start | bytes 270336 | tf_op jit(solution)/shard_map/reduce_scatter | solution.py:41
  265.8 3.2 copy-start.1
  272.1 152.3 %reduce-scatter.11.cloned.1.call-start = ((), (), s32[]{:S(2)}) async-start(), calls=%async_computation.9 | async-start | bytes 294912 | tf_op jit(solution)/shard_map/reduce_scatter | solution.py:42
  272.2 110.9 %copy-start.6 = (f32[16,128]{1,0:T(8,128)S(1)}, f32[16,128]{1,0:T(8,128)}, u32[]{:S(2)}) copy-start(f32[16,128]{1,0:T(8,128)} %reduce-scatter.5.cloned.1.call-done) | copy-start | bytes 24580
  272.2 152.3 %copy-start.3 = (f32[64,128]{1,0:T(8,128)S(1)}, f32[64,128]{1,0:T(8,128)}, u32[]{:S(2)}) copy-start(f32[64,128]{1,0:T(8,128)} %reduce-scatter.7.cloned.1.call-done) | copy-start | bytes 98308
Sparse Core Ops, SparseCore 0:
  75.1 112.9 reduce-scatter.4
  190.6 38.8 reduce-scatter.6
  272.3 110.7 reduce-scatter.8
  385.6 38.8 reduce-scatter.10
